TPU v7x, 32 devices: a whole 2x2x4 slice. The times are simulated.
32 devices in a mesh: groups: 2 (over y), rows: 4 (over x, core), seq: 4 (over z).
Axes of the slice: x: 2, y: 2, z: 4, core: 2. Of those that a mesh axis runs over, the one named last changes fastest.
Arguments:
- activations: bfloat16 [2, 8, 512, 4096], P(None, ('groups', 'rows'), 'seq'), parts along dimension 1, may hold values from -6 to 6
- out_grads: bfloat16 [2, 8, 512, 4096], P(None, ('groups', 'rows'), 'seq'), parts along dimension 1, may hold values from -6 to 6
- lengths: int32 [8], P(('groups', 'rows')), parts along dimension 0, may hold values from 64 to 512
- proj_in: bfloat16 [2, 4096, 64], replicated, may hold values from -0.09375 to 0.09375
- proj_out: bfloat16 [2, 4096, 64], replicated, may hold values from -0.09375 to 0.09375
- basis_in: float32 [2, 64, 64], replicated, may hold values from -0.75 to 0.75
- basis_out: float32 [2, 64, 64], replicated, may hold values from -0.75 to 0.75
- eigen: float32 [2, 64, 64], replicated, may hold values from 10 to 1000
- store: bfloat16 [1024, 8192], P(('groups', 'rows', 'seq')), parts along dimension 0, may hold values from -0.0625 to 0.0625
- candidates: int32 [8, 64], P('groups'), parts along dimension 0, may hold values from 0 to 511
Outputs:
- scores: float32 [1024, 4], P(('groups', 'rows', 'seq')), parts along dimension 0
- picked: float32 [8, 64], P('groups'), parts along dimension 0
There are 2 independent parts, one for each index of `groups`. A program takes and returns all parts, laid end to end along the dimension named above; an argument that names none is the same for every part. Nothing has to cross between parts.
All inputs are finite; a program needn't handle non-finite values.
Results may differ from a plain program's by a relative error of at most 0.005.
Values may be sent and summed in bfloat16 or wider, within the bound.
A program may use at most 64 MiB of HBM per device.

v0:
```python
import jax
import jax.numpy as jnp
from jax import lax
from jax.sharding import PartitionSpec as P

damping = 1.0


def body(
    activations,
    out_grads,
    lengths,
    proj_in,
    proj_out,
    basis_in,
    basis_out,
    eigen,
    store,
    candidates,
):
    nl, bdev, tok, width = activations.shape
    high = lax.Precision.HIGHEST
    offset = lax.axis_index("seq") * tok
    positions = offset + jnp.arange(tok, dtype=jnp.int32)
    mask = (positions[None, :] < lengths[:, None]).astype(jnp.bfloat16)
    pa = jnp.einsum("lbtd,ldr->lbtr", activations, proj_in, preferred_element_type=jnp.float32)
    pg = jnp.einsum("lbtd,ldr->lbtr", out_grads, proj_out, preferred_element_type=jnp.float32)
    pa = pa.astype(jnp.bfloat16) * mask[None, :, :, None]
    pg = pg.astype(jnp.bfloat16) * mask[None, :, :, None]
    local = jnp.einsum("lbto,lbti->lboi", pg, pa, preferred_element_type=jnp.float32)
    total = lax.psum(local, "seq")
    rot = jnp.einsum("loj,lboi,lik->lbjk", basis_out, total, basis_in, precision=high)
    pre = rot / (eigen[:, None] + damping)
    back = jnp.einsum("loj,lbjk,lik->lboi", basis_out, pre, basis_in, precision=high)
    test = jnp.transpose(back, (1, 0, 2, 3)).reshape(bdev, -1).astype(jnp.bfloat16)
    scores = jnp.dot(
        store,
        lax.all_gather(test, "rows", axis=0, tiled=True).T,
        preferred_element_type=jnp.float32,
    )
    rdev = store.shape[0]
    row_start = (lax.axis_index("rows") * lax.axis_size("seq") + lax.axis_index("seq")) * rdev
    local_index = candidates - row_start
    onehot = (local_index[:, :, None] == jnp.arange(rdev, dtype=jnp.int32)[None, None, :]).astype(
        jnp.float32
    )
    picked_local = jnp.einsum("bkr,rb->bk", onehot, scores, precision=high)
    picked = lax.psum(picked_local, ("rows", "seq"))
    return (scores, picked)


def solution(mesh):
    placed = (
        P(None, ("groups", "rows"), "seq", None),
        P(None, ("groups", "rows"), "seq", None),
        P(("groups", "rows")),
        P(),
        P(),
        P(),
        P(),
        P(),
        P(("groups", "rows", "seq"), None),
        P("groups", None),
    )
    return jax.shard_map(
        body,
        mesh=mesh,
        in_specs=placed,
        out_specs=(P(("groups", "rows", "seq"), None), P("groups", None)),
        check_vma=False,
    )
```

profile of v0, /device:TPU:0, one launch (start us, length us, event | category | flops | bytes accessed | tf_op | source)
XLA Modules:
  0.0 67.5 jit_solution(14491491141330753)
XLA Ops:
  0.6 0.0 copy-start
  0.6 0.0 copy-start.1
  1.5 0.8 %copy-done = bf16[2,1,128,4096]{3,2,1,0:T(8,128)(2,1)S(1)} copy-done((bf16[2,1,128,4096]{3,2,1,0:T(8,128)(2,1)S(1)}, bf16[2,1,128,4096]{3,2,1,0:T(8,128)(2,1)}, u32[]{:S(2)}) %copy-start) | copy-done | bytes 2097176
  2.2 2.1 %fusion.16 = bf16[2,128,64]{1,2,0:T(8,128)(2,1)S(1)} fusion(bf16[2,4096,64]{1,2,0:T(8,128)(2,1)} %param.14, bf16[2,1,128,4096]{3,2,1,0:T(8,128)(2,1)S(1)} %copy-done, bf16[128]{0:T(256)(128)(2,1)S(1)} %compare_convert_fusion), kind=kOutput, calls=%fused_computation.10 | convolution fusion | flops 134250496 | bytes 3178752 | tf_op jit(solution)/shard_map/lbtd,ldr->lbtr/dot_general | solution.py:27
  4.3 0.0 copy-done.1
  4.3 0.0 copy-start.2
  4.3 0.0 copy-start.3
  4.3 0.0 copy-start.4
  4.4 0.0 copy-start.5
  4.4 2.7 %fusion.14 = f32[2,64,64]{2,1,0:T(8,128)S(1)} fusion(bf16[2,128,64]{1,2,0:T(8,128)(2,1)S(1)} %fusion.16, bf16[2,4096,64]{1,2,0:T(8,128)(2,1)S(1)} %copy-done.1, bf16[2,1,128,4096]{3,2,1,0:T(8,128)(2,1)} %param.10, bf16[128]{0:T(256)(128)(2,1)S(1)} %compare_convert_fusion), kind=kOutput, calls=%fused_computation.9 | convolution fusion | flops 136347648 | bytes 3211520 | tf_op jit(solution)/shard_map/lbto,lbti->lboi/dot_general | solution.py:30
  7.0 21.5 %psum.14 = f32[2,64,64]{2,1,0:T(8,128)S(1)} all-reduce(f32[2,64,64]{2,1,0:T(8,128)S(1)} %fusion.14), channel_id=1, replica_groups=mesh['groups'=2,'rows'=4,'seq'=4] {'seq'}, use_global_device_ids=true, to_apply=%region_0.0 | all-reduce | flops 8192 | bytes 65536 | tf_op jit(solution)/shard_map/psum | solution.py:31
  28.6 0.0 copy-done.2
  28.6 0.3 fusion.25
  28.9 0.0 copy-done.3
  28.9 0.0 copy-done.4
  28.9 0.2 convolution_divide_fusion
  29.1 0.2 fusion.26
  29.3 0.2 convolution_convert_fusion
  29.5 0.1 reshape.69
  29.6 5.4 %all-gather = bf16[4,1,8192]{2,1,0:T(2,128)(2,1)S(1)} all-gather(bf16[1,1,8192]{2,1,0:T(2,128)(2,1)S(1)} %reshape.69), channel_id=1, replica_groups=mesh['groups'=2,'rows'=4,'seq'=4] {'rows'}, dimensions={0}, use_global_device_ids=true | all-gather | bytes 81920 | tf_op jit(solution)/shard_map/all_gather | solution.py:38
  35.0 1.3 %fusion.20 = f32[4,32]{1,0:T(4,128)S(1)} fusion(bf16[32,8192]{1,0:T(8,128)(2,1)} %param.18, bf16[4,1,8192]{2,1,0:T(2,128)(2,1)S(1)} %all-gather), kind=kOutput, calls=%fused_computation.13 | convolution fusion | flops 2097152 | bytes 590336 | tf_op jit(solution)/shard_map/dot_general | solution.py:36
  36.3 0.0 copy-start.6
  36.3 0.0 copy-done.5
  36.3 0.3 fusion.19
  36.6 30.9 %psum.15 = f32[4,64]{1,0:T(4,128)} all-reduce(f32[4,64]{1,0:T(4,128)S(1)} %bitcast.41), channel_id=1, replica_groups=mesh['groups'=2,'rows'=4,'seq'=4] {'rows','seq'}, use_global_device_ids=true, to_apply=%region_1.0 | all-reduce | flops 256 | bytes 2048 | tf_op jit(solution)/shard_map/psum | solution.py:48
  67.5 0.0 copy-done.6
  (2 shorter events, 0.0 us)
Async XLA Ops:
  0.6 1.6 %copy-start = (bf16[2,1,128,4096]{3,2,1,0:T(8,128)(2,1)S(1)}, bf16[2,1,128,4096]{3,2,1,0:T(8,128)(2,1)}, u32[]{:S(2)}) copy-start(bf16[2,1,128,4096]{3,2,1,0:T(8,128)(2,1)} %param.11) | copy-start | bytes 6291460
  0.6 3.7 %copy-start.1 = (bf16[2,4096,64]{1,2,0:T(8,128)(2,1)S(1)}, bf16[2,4096,64]{1,2,0:T(8,128)(2,1)}, u32[]{:S(2)}) copy-start(bf16[2,4096,64]{1,2,0:T(8,128)(2,1)} %param.13) | copy-start | bytes 3145732
  4.3 24.2 %copy-start.2 = (f32[2,64,64]{2,1,0:T(8,128)S(1)}, f32[2,64,64]{2,1,0:T(8,128)}, u32[]{:S(2)}) copy-start(f32[2,64,64]{2,1,0:T(8,128)} %param.16) | copy-start | bytes 98308
  4.3 24.5 %copy-start.3 = (f32[2,64,64]{2,1,0:T(8,128)S(1)}, f32[2,64,64]{2,1,0:T(8,128)}, u32[]{:S(2)}) copy-start(f32[2,64,64]{2,1,0:T(8,128)} %param.15) | copy-start | bytes 98308
  4.3 24.5 %copy-start.4 = (f32[2,64,64]{2,1,0:T(8,128)S(1)}, f32[2,64,64]{2,1,0:T(8,128)}, u32[]{:S(2)}) copy-start(f32[2,64,64]{2,1,0:T(8,128)} %param.17) | copy-start | bytes 98308
  4.4 32.0 %copy-start.5 = (s32[4,64]{1,0:T(4,128)S(1)}, s32[4,64]{1,0:T(4,128)}, u32[]{:S(2)}) copy-start(s32[4,64]{1,0:T(4,128)} %param.19) | copy-start | bytes 3076
  36.3 31.2 %copy-start.6 = (f32[4,32]{1,0:T(4,128)}, f32[4,32]{1,0:T(4,128)S(1)}, u32[]{:S(2)}) copy-start(f32[4,32]{1,0:T(4,128)S(1)} %fusion.20) | copy-start | bytes 1540
where the time goes:
time: 67.8 us; the launch traced here: 67.5 us
  blocking collectives  57.9 us (85%)
  matrix products  7.18 us (11%)
  between operations  1.57 us (2%)
  local copies, waits for them, and re-layouts  0.91 us (1%)
    psum x1, blocking collectives, body(): picked = lax.psum(picked_local, ('rows', 'seq'))  30.9 us
    psum x1, blocking collectives, body(): total = lax.psum(local, 'seq')  21.5 us
    all_gather x1, blocking collectives, body(): lax.all_gather(test, 'rows', axis=0, tiled=True)  5.43 us
    dot_general x1, matrix products, body(): jnp.einsum('lbto,lbti->lboi', pg, pa, preferred_element_type=jnp.float32)  2.65 us
    dot_general x1, matrix products, body(): jnp.einsum('lbtd,ldr->lbtr', out_grads, proj_out, preferred_element_type=...  2.06 us

commit v1 on v0

--- a/solution.py
+++ b/solution.py
@@ -2,6 +2,7 @@
 import jax.numpy as jnp
 from jax import lax
 from jax.sharding import PartitionSpec as P
+from jax.lax import psum
 
 damping = 1.0
 
@@ -45,7 +46,7 @@
         jnp.float32
     )
     picked_local = jnp.einsum("bkr,rb->bk", onehot, scores, precision=high)
-    picked = lax.psum(picked_local, ("rows", "seq"))
+    picked = psum(psum(picked_local, "seq"), "rows")
     return (scores, picked)
 
 

time: 67.8 us -> 51.5 us (0.76)
  blocking collectives: 57.9 us -> 41.5 us
    psum x1 -> x2, blocking collectives: 30.9 us -> 14.6 us  [body(): picked = psum(psum(picked_local, 'seq'), 'rows')]
where the time goes in v1:
time: 51.5 us; the launch traced here: 51.2 us
  blocking collectives  41.5 us (81%)
  matrix products  7.18 us (14%)
  between operations  1.57 us (3%)
  local copies, waits for them, and re-layouts  0.91 us (2%)
    psum x1, blocking collectives, body(): total = lax.psum(local, 'seq')  21.5 us
    psum x2, blocking collectives, body(): picked = psum(psum(picked_local, 'seq'), 'rows')  14.6 us
    all_gather x1, blocking collectives, body(): lax.all_gather(test, 'rows', axis=0, tiled=True)  5.43 us
    dot_general x1, matrix products, body(): jnp.einsum('lbto,lbti->lboi', pg, pa, preferred_element_type=jnp.float32)  2.65 us
    dot_general x1, matrix products, body(): jnp.einsum('lbtd,ldr->lbtr', out_grads, proj_out, preferred_element_type=...  2.06 us
    dot_general x1, matrix products, body(): jnp.dot(store, lax.all_gather(test, 'rows', axis=0, tiled=True).T, prefer...  1.29 us

profile of v1, /device:TPU:0, one launch (start us, length us, event | category | flops | bytes accessed | tf_op | source)
XLA Modules:
  0.0 51.2 jit_solution(15397679134452369405)
XLA Ops:
  0.6 0.0 copy-start
  0.6 0.0 copy-start.1
  1.5 0.8 %copy-done = bf16[2,1,128,4096]{3,2,1,0:T(8,128)(2,1)S(1)} copy-done((bf16[2,1,128,4096]{3,2,1,0:T(8,128)(2,1)S(1)}, bf16[2,1,128,4096]{3,2,1,0:T(8,128)(2,1)}, u32[]{:S(2)}) %copy-start) | copy-done | bytes 2097176
  2.2 2.1 %fusion.16 = bf16[2,128,64]{1,2,0:T(8,128)(2,1)S(1)} fusion(bf16[2,4096,64]{1,2,0:T(8,128)(2,1)} %param.14, bf16[2,1,128,4096]{3,2,1,0:T(8,128)(2,1)S(1)} %copy-done, bf16[128]{0:T(256)(128)(2,1)S(1)} %compare_convert_fusion), kind=kOutput, calls=%fused_computation.10 | convolution fusion | flops 134250496 | bytes 3178752 | tf_op jit(solution)/shard_map/lbtd,ldr->lbtr/dot_general | solution.py:28
  4.3 0.0 copy-done.1
  4.3 0.0 copy-start.2
  4.3 0.0 copy-start.3
  4.3 0.0 copy-start.4
  4.4 0.0 copy-start.5
  4.4 2.7 %fusion.14 = f32[2,64,64]{2,1,0:T(8,128)S(1)} fusion(bf16[2,128,64]{1,2,0:T(8,128)(2,1)S(1)} %fusion.16, bf16[2,4096,64]{1,2,0:T(8,128)(2,1)S(1)} %copy-done.1, bf16[2,1,128,4096]{3,2,1,0:T(8,128)(2,1)} %param.10, bf16[128]{0:T(256)(128)(2,1)S(1)} %compare_convert_fusion), kind=kOutput, calls=%fused_computation.9 | convolution fusion | flops 136347648 | bytes 3211520 | tf_op jit(solution)/shard_map/lbto,lbti->lboi/dot_general | solution.py:31
  7.0 21.5 %psum.21 = f32[2,64,64]{2,1,0:T(8,128)S(1)} all-reduce(f32[2,64,64]{2,1,0:T(8,128)S(1)} %fusion.14), channel_id=1, replica_groups=mesh['groups'=2,'rows'=4,'seq'=4] {'seq'}, use_global_device_ids=true, to_apply=%region_0.0 | all-reduce | flops 8192 | bytes 65536 | tf_op jit(solution)/shard_map/psum | solution.py:32
  28.6 0.0 copy-done.2
  28.6 0.3 fusion.25
  28.9 0.0 copy-done.3
  28.9 0.0 copy-done.4
  28.9 0.2 convolution_divide_fusion
  29.1 0.2 fusion.26
  29.3 0.2 convolution_convert_fusion
  29.5 0.1 reshape.69
  29.6 5.4 %all-gather = bf16[4,1,8192]{2,1,0:T(2,128)(2,1)S(1)} all-gather(bf16[1,1,8192]{2,1,0:T(2,128)(2,1)S(1)} %reshape.69), channel_id=1, replica_groups=mesh['groups'=2,'rows'=4,'seq'=4] {'rows'}, dimensions={0}, use_global_device_ids=true | all-gather | bytes 81920 | tf_op jit(solution)/shard_map/all_gather | solution.py:39
  35.0 1.3 %fusion.20 = f32[4,32]{1,0:T(4,128)S(1)} fusion(bf16[32,8192]{1,0:T(8,128)(2,1)} %param.18, bf16[4,1,8192]{2,1,0:T(2,128)(2,1)S(1)} %all-gather), kind=kOutput, calls=%fused_computation.13 | convolution fusion | flops 2097152 | bytes 590336 | tf_op jit(solution)/shard_map/dot_general | solution.py:37
  36.3 0.0 copy-start.6
  36.3 0.0 copy-done.5
  36.3 0.3 fusion.19
  36.6 8.4 %psum.22 = f32[4,64]{1,0:T(4,128)S(1)} all-reduce(f32[4,64]{1,0:T(4,128)S(1)} %bitcast.41), channel_id=1, replica_groups=mesh['groups'=2,'rows'=4,'seq'=4] {'seq'}, use_global_device_ids=true, to_apply=%region_1.0 | all-reduce | flops 256 | bytes 2048 | tf_op jit(solution)/shard_map/psum | solution.py:49
  45.0 6.2 %psum.23 = f32[4,64]{1,0:T(4,128)} all-reduce(f32[4,64]{1,0:T(4,128)S(1)} %psum.22), channel_id=1, replica_groups=mesh['groups'=2,'rows'=4,'seq'=4] {'rows'}, use_global_device_ids=true, to_apply=%region_2.0 | all-reduce | flops 256 | bytes 2048 | tf_op jit(solution)/shard_map/psum | solution.py:49
  51.2 0.0 copy-done.6
  (2 shorter events, 0.0 us)
Async XLA Ops:
  0.6 1.6 %copy-start = (bf16[2,1,128,4096]{3,2,1,0:T(8,128)(2,1)S(1)}, bf16[2,1,128,4096]{3,2,1,0:T(8,128)(2,1)}, u32[]{:S(2)}) copy-start(bf16[2,1,128,4096]{3,2,1,0:T(8,128)(2,1)} %param.11) | copy-start | bytes 6291460
  0.6 3.7 %copy-start.1 = (bf16[2,4096,64]{1,2,0:T(8,128)(2,1)S(1)}, bf16[2,4096,64]{1,2,0:T(8,128)(2,1)}, u32[]{:S(2)}) copy-start(bf16[2,4096,64]{1,2,0:T(8,128)(2,1)} %param.13) | copy-start | bytes 3145732
  4.3 24.2 %copy-start.2 = (f32[2,64,64]{2,1,0:T(8,128)S(1)}, f32[2,64,64]{2,1,0:T(8,128)}, u32[]{:S(2)}) copy-start(f32[2,64,64]{2,1,0:T(8,128)} %param.16) | copy-start | bytes 98308
  4.3 24.5 %copy-start.3 = (f32[2,64,64]{2,1,0:T(8,128)S(1)}, f32[2,64,64]{2,1,0:T(8,128)}, u32[]{:S(2)}) copy-start(f32[2,64,64]{2,1,0:T(8,128)} %param.15) | copy-start | bytes 98308
  4.3 24.5 %copy-start.4 = (f32[2,64,64]{2,1,0:T(8,128)S(1)}, f32[2,64,64]{2,1,0:T(8,128)}, u32[]{:S(2)}) copy-start(f32[2,64,64]{2,1,0:T(8,128)} %param.17) | copy-start | bytes 98308
  4.4 32.0 %copy-start.5 = (s32[4,64]{1,0:T(4,128)S(1)}, s32[4,64]{1,0:T(4,128)}, u32[]{:S(2)}) copy-start(s32[4,64]{1,0:T(4,128)} %param.19) | copy-start | bytes 3076
  36.3 14.9 %copy-start.6 = (f32[4,32]{1,0:T(4,128)}, f32[4,32]{1,0:T(4,128)S(1)}, u32[]{:S(2)}) copy-start(f32[4,32]{1,0:T(4,128)S(1)} %fusion.20) | copy-start | bytes 1540
